TPU v7x, 32 devices: a whole 2x2x4 slice. The times are simulated.
32 devices in a mesh: dp: 16 (over z, y, x), space: 2 (over core).
Axes of the slice: x: 2, y: 2, z: 4, core: 2. Of those that a mesh axis runs over, the one named last changes fastest.
Arguments:
- images: bfloat16 [16, 16, 288, 256], P('dp', 'space'), may hold values from -12 to 12
- w_reduce: bfloat16 [256, 64], replicated, may hold values from -0.375 to 0.375
- w_dilated: bfloat16 [3, 3, 64, 64], replicated, may hold values from -0.25 to 0.25
- w_expand: bfloat16 [64, 256], replicated, may hold values from -0.75 to 0.75
- gain_one: float32 [64], replicated, may hold values from 0.25 to 1.75
- shift_one: float32 [64], replicated, may hold values from -3 to 3
- gain_two: float32 [64], replicated, may hold values from 0.25 to 1.75
- shift_two: float32 [64], replicated, may hold values from -3 to 3
- gain_three: float32 [256], replicated, may hold values from 0.25 to 1.75
- shift_three: float32 [256], replicated, may hold values from -3 to 3
- cotangent: bfloat16 [16, 16, 288, 256], P('dp', 'space'), may hold values from -6 to 6
Outputs:
- result: bfloat16 [16, 16, 288, 256], P('dp', 'space')
- grad_images: bfloat16 [16, 16, 288, 256], P('dp', 'space')
- grad_reduce: float32 [256, 64], replicated
- grad_dilated: float32 [3, 3, 64, 64], replicated
- grad_expand: float32 [64, 256], replicated
- grad_gain_one: float32 [64], replicated
- grad_shift_one: float32 [64], replicated
- grad_gain_two: float32 [64], replicated
- grad_shift_two: float32 [64], replicated
- grad_gain_three: float32 [256], replicated
- grad_shift_three: float32 [256], replicated
All inputs are finite; a program needn't handle non-finite values.
Results may differ from a plain program's by a relative error of at most 0.012.
Values may be sent and summed in bfloat16 or wider, within the bound.
No kernel may reach another device: no remote copies, remote signals or barrier semaphores. Data moves between devices by JAX's collectives and lax.ppermute only.
A program may use at most 64 MiB of HBM per device.

v0:
```python
import jax
import jax.numpy as jnp
from jax import lax
from jax.sharding import PartitionSpec as P

epsilon = 1e-05


def extended(block, sides, width):
    for axis, dim in sides:
        count = lax.axis_size(axis)
        forward = [(i, i + 1) for i in range(count - 1)]
        backward = [(target, source) for source, target in forward]
        low = lax.ppermute(
            lax.slice_in_dim(block, block.shape[dim] - width, None, axis=dim), axis, forward
        )
        high = lax.ppermute(lax.slice_in_dim(block, 0, width, axis=dim), axis, backward)
        block = jnp.concatenate([low, block, high], axis=dim)
    return block


def smooth_act(value):
    return value * jax.nn.sigmoid(value)


def smooth_slope(value):
    sig = jax.nn.sigmoid(value)
    return sig * (1.0 + value * (1.0 - sig))


def normalize(pre, gain, shift, count):
    average = lax.psum(jnp.sum(pre, 0), "space") / count
    centred = pre - average
    variance = lax.psum(jnp.sum(centred * centred, 0), "space") / count
    inv_std = lax.rsqrt(variance + epsilon)
    normed = centred * inv_std
    return (normed, inv_std, gain * normed + shift)


def backnorm(grad, normed, inv_std, gain, count):
    local_sum = jnp.sum(grad, 0)
    local_cross = jnp.sum(grad * normed, 0)
    grad_sum, grad_cross = lax.psum((local_sum, local_cross), "space")
    back = (gain * inv_std * (grad - grad_sum / count - normed * grad_cross / count)).astype(
        jnp.bfloat16
    )
    return (back, local_cross, local_sum)


def dilated(padded, kernel, rows, cols):
    output = jnp.zeros((rows * cols, kernel.shape[3]), jnp.float32)
    for tap_row in range(3):
        for tap_col in range(3):
            window = padded[
                2 * tap_row : 2 * tap_row + rows, 2 * tap_col : 2 * tap_col + cols
            ].reshape(rows * cols, -1)
            output = output + jnp.dot(
                window, kernel[tap_row, tap_col], preferred_element_type=jnp.float32
            )
    return output


def contract(left, right):
    return lax.dot_general(
        left, right, (((0,), (0,)), ((), ())), preferred_element_type=jnp.float32
    )


def shards(
    images,
    w_reduce,
    w_dilated,
    w_expand,
    gain_one,
    shift_one,
    gain_two,
    shift_two,
    gain_three,
    shift_three,
    cotangent,
):
    rows, cols, chans = (images.shape[1], images.shape[2], images.shape[3])
    mids = w_reduce.shape[1]
    pixels = rows * cols
    count = float(pixels * lax.axis_size("space"))
    flat_in = images.reshape(pixels, chans)
    pre_one = jnp.dot(flat_in, w_reduce, preferred_element_type=jnp.float32)
    normed_one, istd_one, out_one = normalize(pre_one, gain_one, shift_one, count)
    act_one = smooth_act(out_one).astype(jnp.bfloat16)
    edged_one = extended(act_one.reshape(rows, cols, mids), (("space", 0),), 2)
    padded_one = jnp.pad(edged_one, ((0, 0), (2, 2), (0, 0)))
    pre_two = dilated(padded_one, w_dilated, rows, cols)
    normed_two, istd_two, out_two = normalize(pre_two, gain_two, shift_two, count)
    act_two = smooth_act(out_two).astype(jnp.bfloat16)
    pre_three = jnp.dot(act_two, w_expand, preferred_element_type=jnp.float32)
    normed_three, istd_three, out_three = normalize(pre_three, gain_three, shift_three, count)
    summed = out_three + flat_in.astype(jnp.float32)
    result = smooth_act(summed).astype(jnp.bfloat16)
    grad_three = cotangent.reshape(pixels, chans).astype(jnp.float32) * smooth_slope(summed)
    dh_three, gg_three, gs_three = backnorm(grad_three, normed_three, istd_three, gain_three, count)
    gw_expand = contract(act_two, dh_three)
    back_two = lax.dot_general(
        dh_three, w_expand, (((1,), (1,)), ((), ())), preferred_element_type=jnp.float32
    )
    grad_two = back_two * smooth_slope(out_two)
    dh_two, gg_two, gs_two = backnorm(grad_two, normed_two, istd_two, gain_two, count)
    taps = []
    for tap_row in range(3):
        for tap_col in range(3):
            window = padded_one[
                2 * tap_row : 2 * tap_row + rows, 2 * tap_col : 2 * tap_col + cols
            ].reshape(pixels, mids)
            taps.append(contract(window, dh_two))
    gw_dilated = jnp.stack(taps).reshape(3, 3, mids, mids)
    edged_back = extended(dh_two.reshape(rows, cols, mids), (("space", 0),), 2)
    padded_back = jnp.pad(edged_back, ((0, 0), (2, 2), (0, 0)))
    flipped = jnp.transpose(w_dilated[::-1, ::-1], (0, 1, 3, 2))
    grad_one = dilated(padded_back, flipped, rows, cols) * smooth_slope(out_one)
    dh_one, gg_one, gs_one = backnorm(grad_one, normed_one, istd_one, gain_one, count)
    gw_reduce = contract(flat_in, dh_one)
    back_in = lax.dot_general(
        dh_one, w_reduce, (((1,), (1,)), ((), ())), preferred_element_type=jnp.float32
    )
    grad_images = (back_in + grad_three).astype(jnp.bfloat16).reshape(1, rows, cols, chans)
    batch = float(lax.axis_size("dp"))
    parts_list = (
        gw_reduce,
        gw_dilated,
        gw_expand,
        gg_one,
        gs_one,
        gg_two,
        gs_two,
        gg_three,
        gs_three,
    )
    flat_grads = jnp.concatenate([item.reshape(-1) for item in parts_list])
    length = flat_grads.shape[0]
    groups = lax.axis_size("space")
    padded_len = (length + groups - 1) // groups * groups
    flat_grads = jnp.pad(flat_grads, (0, padded_len - length))
    share = lax.psum_scatter(
        flat_grads.astype(jnp.bfloat16), "space", scatter_dimension=0, tiled=True
    ).astype(jnp.float32)
    share = lax.psum(share, "dp")
    whole = lax.all_gather(share.astype(jnp.bfloat16), "space", axis=0, tiled=True).astype(
        share.dtype
    )
    summed_parts = []
    offset = 0
    for item in parts_list:
        summed_parts.append(whole[offset : offset + item.size].reshape(item.shape))
        offset = offset + item.size
    grads = [item / batch for item in summed_parts]
    return (
        result.reshape(1, rows, cols, chans),
        grad_images,
        grads[0],
        grads[1],
        grads[2],
        grads[3],
        grads[4],
        grads[5],
        grads[6],
        grads[7],
        grads[8],
    )


def solution(mesh):
    placed = (
        P("dp", "space", None, None),
        P(),
        P(),
        P(),
        P(),
        P(),
        P(),
        P(),
        P(),
        P(),
        P("dp", "space", None, None),
    )
    return jax.shard_map(
        shards,
        mesh=mesh,
        in_specs=placed,
        out_specs=(
            P("dp", "space", None, None),
            P("dp", "space", None, None),
            P(),
            P(),
            P(),
            P(),
            P(),
            P(),
            P(),
            P(),
            P(),
        ),
        check_vma=False,
    )
```

profile of v0, /device:TPU:0, one launch (start us, length us, event | category | flops | bytes accessed | tf_op | source)
XLA Modules:
  0.0 222.0 jit_solution(6507126635642277111)
XLA Ops:
  7.3 1.9 fusion.59
  9.2 2.6 %psum.91 = f32[64]{0:T(128)S(1)} all-reduce(f32[64]{0:T(128)S(1)} %get-tuple-element.81), channel_id=1, replica_groups=mesh['dp'=16,'space'=2] {'space'}, use_global_device_ids=true, to_apply=%region_1.0 | all-reduce | flops 64 | bytes 512 | tf_op jit(solution)/shard_map/psum | solution.py:32
  12.1 2.5 %psum.92 = f32[64]{0:T(128)S(1)} all-reduce(f32[64]{0:T(128)S(1)} %multiply_reduce_fusion.5), channel_id=1, replica_groups=mesh['dp'=16,'space'=2] {'space'}, use_global_device_ids=true, to_apply=%region_3.0 | all-reduce | flops 64 | bytes 512 | tf_op jit(solution)/shard_map/psum | solution.py:34
  16.3 2.3 %collective-permute-start = (bf16[2,288,64]{1,0,2:T(2,128)(2,1)S(1)}, bf16[2,288,64]{1,0,2:T(2,128)(2,1)S(1)}, u32[]{:S(2)}, u32[]{:S(2)}) collective-permute-start(bf16[2,288,64]{1,0,2:T(2,128)(2,1)S(1)} %slice.191), channel_id=1, source_target_pairs={{0,1},{2,3},{4,5},{6,7},{8,9},{10,11},{12,13},{14,15},{16,17},{18,... | collective-permute-start | bytes 221192 | tf_op jit(solution)/shard_map/ppermute | solution.py:14
  23.6 1.8 fusion.56
  42.2 3.3 %psum.93 = f32[64]{0:T(128)S(1)} all-reduce(f32[64]{0:T(128)S(1)} %get-tuple-element.83), channel_id=1, replica_groups=mesh['dp'=16,'space'=2] {'space'}, use_global_device_ids=true, to_apply=%region_5.6 | all-reduce | flops 64 | bytes 512 | tf_op jit(solution)/shard_map/psum | solution.py:32
  45.7 2.5 %psum.94 = f32[64]{0:T(128)S(1)} all-reduce(f32[64]{0:T(128)S(1)} %multiply_reduce_fusion.4), channel_id=1, replica_groups=mesh['dp'=16,'space'=2] {'space'}, use_global_device_ids=true, to_apply=%region_7.8 | all-reduce | flops 64 | bytes 512 | tf_op jit(solution)/shard_map/psum | solution.py:34
  48.2 1.9 fusion.61
  50.1 2.5 %psum.95 = f32[256]{0:T(256)S(1)} all-reduce(f32[256]{0:T(256)S(1)} %get-tuple-element.85), channel_id=1, replica_groups=mesh['dp'=16,'space'=2] {'space'}, use_global_device_ids=true, to_apply=%region_9.10 | all-reduce | flops 256 | bytes 2048 | tf_op jit(solution)/shard_map/psum | solution.py:32
  52.9 2.6 %psum.96 = f32[256]{0:T(256)S(1)} all-reduce(f32[256]{0:T(256)S(1)} %multiply_reduce_fusion.1), channel_id=1, replica_groups=mesh['dp'=16,'space'=2] {'space'}, use_global_device_ids=true, to_apply=%region_11.12 | all-reduce | flops 256 | bytes 2048 | tf_op jit(solution)/shard_map/psum | solution.py:34
  55.6 5.1 %fusion.52 = (f32[256]{0:T(256)S(1)}, f32[256]{0:T(256)S(1)}, f32[2304,256]{1,0:T(8,128)}, bf16[2304,256]{1,0:T(8,128)(2,1)}) fusion(f32[256]{0:T(256)S(1)} %get-tuple-element.76, f32[2304,256]{1,0:T(8,128)S(1)} %get-tuple-element.86, f32[256]{0:T(256)S(1)} %broadcast_multiply_fusion.1, bf16[1,8,288,256]{3,2,1,0:T(8,128)(2,1)} %param.11, ...), kind=kLoop, calls=%fused_computation.141 | loop fusion | flops 11795968 | bytes 8263680 | tf_op jit(solution)/shard_map/reduce_sum | solution.py:41
  60.6 2.5 %all-reduce.5 = (f32[256]{0:T(256)S(1)}, f32[256]{0:T(256)S(1)}) all-reduce(f32[256]{0:T(256)S(1)} %get-tuple-element.34, f32[256]{0:T(256)S(1)} %get-tuple-element.33), channel_id=1, replica_groups=mesh['dp'=16,'space'=2] {'space'}, use_global_device_ids=true, to_apply=%region_15.16 | all-reduce | flops 512 | bytes 4096 | tf_op jit(solution)/shard_map/psum | solution.py:43
  63.1 2.3 %multiply_convert_fusion = bf16[2304,256]{1,0:T(8,128)(2,1)S(1)} fusion(f32[2304,256]{1,0:T(8,128)} %get-tuple-element.45, f32[2304,256]{1,0:T(8,128)S(1)} %get-tuple-element.86, f32[256]{0:T(256)S(1)} %get-tuple-element.43, f32[256]{0:T(256)S(1)} %broadcast_multiply_fusion, f32[256]{0:T(256)S(1)} %get-tuple-element.75, f32[256]{0:T(256)S(1)} %get-tuple-element.76, ...), kind=kLoop, calls=%fused_computation.23 | loop fusion | flops 4718592 | bytes 5903360 | tf_op jit(solution)/shard_map/convert_element_type | solution.py:44
  67.3 2.6 %all-reduce.4 = (f32[64]{0:T(128)S(1)}, f32[64]{0:T(128)S(1)}) all-reduce(f32[64]{0:T(128)S(1)} %get-tuple-element.38, f32[64]{0:T(128)S(1)} %get-tuple-element.37), channel_id=1, replica_groups=mesh['dp'=16,'space'=2] {'space'}, use_global_device_ids=true, to_apply=%region_19.20 | all-reduce | flops 128 | bytes 1024 | tf_op jit(solution)/shard_map/psum | solution.py:43
  69.9 1.5 multiply_convert_fusion.3
  73.6 2.3 %collective-permute-start.2 = (bf16[2,288,64]{1,0,2:T(2,128)(2,1)S(1)}, bf16[2,288,64]{1,0,2:T(2,128)(2,1)S(1)}, u32[]{:S(2)}, u32[]{:S(2)}) collective-permute-start(bf16[2,288,64]{1,0,2:T(2,128)(2,1)S(1)} %slice.212), channel_id=1, source_target_pairs={{0,1},{2,3},{4,5},{6,7},{8,9},{10,11},{12,13},{14,15},{16,17},{18,... | collective-permute-start | bytes 221192 | tf_op jit(solution)/shard_map/ppermute | solution.py:14
  84.3 1.5 fusion.55
  94.8 3.6 %all-reduce.3 = (f32[64]{0:T(128)S(1)}, f32[64]{0:T(128)S(1)}) all-reduce(f32[64]{0:T(128)S(1)} %get-tuple-element.36, f32[64]{0:T(128)S(1)} %get-tuple-element.35), channel_id=1, replica_groups=mesh['dp'=16,'space'=2] {'space'}, use_global_device_ids=true, to_apply=%region_23.24 | all-reduce | flops 128 | bytes 1024 | tf_op jit(solution)/shard_map/psum | solution.py:43
  99.9 1.6 fusion.5
  101.7 6.3 %concatenate.28 = bf16[70400]{0:T(1024)(128)(2,1)} concatenate(bf16[16384]{0:T(1024)(128)(2,1)S(1)} %reshape.180, bf16[36864]{0:T(1024)(128)(2,1)S(1)} %copy-done.27, bf16[16384]{0:T(1024)(128)(2,1)S(1)} %bitcast.206, bf16[64]{0:T(256)(128)(2,1)S(1)} %convert.77, bf16[64]{0:T(256)(128)(2,1)S(1)} %convert.78, bf16[64]{0:T(256)(128)(2,1)S(1)} %copy-done.39, ...), dimensions={0} | concatenate | bytes 281600 | tf_op jit(solution)/shard_map/concatenate | solution.py:137
  108.1 1.5 fusion
  109.6 18.9 %all-reduce.9.cloned.1.call-done = bf16[70400]{0:T(1024)(128)(2,1)} async-done(((bf16[70400]{0:T(1024)(128)(2,1)}), bf16[70400]{0:T(1024)(128)(2,1)}) %all-reduce.9.cloned.1.call-update) | async-done | bytes 140816
  129.5 78.9 %all-reduce.10 = bf16[35200]{0:T(1024)(128)(2,1)S(1)} all-reduce(f32[35200]{0:T(1024)S(1)} %dynamic-slice_convert_fusion), channel_id=1, replica_groups=mesh['dp'=16,'space'=2] {'dp'}, use_global_device_ids=true, to_apply=%region_25.26 | all-reduce | flops 35200 | bytes 211200 | tf_op jit(solution)/shard_map/psum | solution.py:145
  208.5 2.0 all-gather
  (195 shorter events, 51.8 us)
Async XLA Ops:
  7.2 41.0 %copy-start = (bf16[64,256]{1,0:T(8,128)(2,1)S(1)}, bf16[64,256]{1,0:T(8,128)(2,1)}, u32[]{:S(2)}) copy-start(bf16[64,256]{1,0:T(8,128)(2,1)} %param.14) | copy-start | bytes 98308
  7.2 13.4 %copy-start.45 = (u32[32]{0:T(128)S(1)}, u32[32]{0:T(128)}, u32[]{:S(2)}) copy-start(u32[32]{0:T(128)} %constant.51) | copy-start | bytes 388
  7.2 7.3 %copy-start.34 = (f32[64]{0:T(128)S(1)}, f32[64]{0:T(128)}, u32[]{:S(2)}) copy-start(f32[64]{0:T(128)} %param.15) | copy-start | bytes 772
  7.2 8.4 %copy-start.37 = (f32[64]{0:T(128)S(1)}, f32[64]{0:T(128)}, u32[]{:S(2)}) copy-start(f32[64]{0:T(128)} %param.16) | copy-start | bytes 772
  7.2 14.6 %copy-start.25 = (bf16[3,3,64,64]{3,2,1,0:T(8,128)(2,1)S(1)}, bf16[3,3,64,64]{3,2,1,0:T(8,128)(2,1)}, u32[]{:S(2)}) copy-start(bf16[3,3,64,64]{3,2,1,0:T(8,128)(2,1)} %param.13) | copy-start | bytes 221188
  7.2 121.3 %all-reduce.9.cloned.1.call-start = ((), (), s32[]{:S(2)}) async-start(), calls=%async_computation | async-start | bytes 282624
  16.3 6.3 %collective-permute-start = (bf16[2,288,64]{1,0,2:T(2,128)(2,1)S(1)}, bf16[2,288,64]{1,0,2:T(2,128)(2,1)S(1)}, u32[]{:S(2)}, u32[]{:S(2)}) collective-permute-start(bf16[2,288,64]{1,0,2:T(2,128)(2,1)S(1)} %slice.191), channel_id=1, source_target_pairs={{0,1},{2,3},{4,5},{6,7},{8,9},{10,11},{12,13},{14,15},{16,17},{18,... | collective-permute-start | bytes 221192 | tf_op jit(solution)/shard_map/ppermute | solution.py:14
  18.7 3.9 %collective-permute-start.1 = (bf16[2,288,64]{1,0,2:T(2,128)(2,1)S(1)}, bf16[2,288,64]{1,0,2:T(2,128)(2,1)S(1)}, u32[]{:S(2)}, u32[]{:S(2)}) collective-permute-start(bf16[2,288,64]{1,0,2:T(2,128)(2,1)S(1)} %slice.193), channel_id=1, source_target_pairs={{1,0},{3,2},{5,4},{7,6},{9,8},{11,10},{13,12},{15,14},{17,16},{19,... | collective-permute-start | bytes 221192 | tf_op jit(solution)/shard_map/ppermute | solution.py:17
  25.7 5.7 %copy-start.9 = (bf16[2304,64]{0,1:T(8,128)(2,1)}, bf16[2304,64]{0,1:T(8,128)(2,1)S(1)}, u32[]{:S(2)}) copy-start(bf16[2304,64]{0,1:T(8,128)(2,1)S(1)} %reshape.161) | copy-start | bytes 884740
  27.5 6.1 %copy-start.15 = (bf16[2304,64]{0,1:T(8,128)(2,1)}, bf16[2304,64]{0,1:T(8,128)(2,1)S(1)}, u32[]{:S(2)}) copy-start(bf16[2304,64]{0,1:T(8,128)(2,1)S(1)} %reshape.162) | copy-start | bytes 884740
  40.0 8.2 %copy-start.43 = (f32[64]{0:T(128)S(1)}, f32[64]{0:T(128)}, u32[]{:S(2)}) copy-start(f32[64]{0:T(128)} %param.17) | copy-start | bytes 772
  40.0 8.2 %copy-start.44 = (f32[64]{0:T(128)S(1)}, f32[64]{0:T(128)}, u32[]{:S(2)}) copy-start(f32[64]{0:T(128)} %param.18) | copy-start | bytes 772
  42.2 6.0 %copy-start.2 = (f32[2304,64]{0,1:T(8,128)}, f32[2304,64]{0,1:T(8,128)S(1)}, u32[]{:S(2)}) copy-start(f32[2304,64]{0,1:T(8,128)S(1)} %get-tuple-element.84) | copy-start | bytes 1769476
  48.2 7.4 %copy-start.33 = (f32[256]{0:T(256)S(1)}, f32[256]{0:T(256)}, u32[]{:S(2)}) copy-start(f32[256]{0:T(256)} %param.19) | copy-start | bytes 3076
  48.2 7.4 %copy-start.36 = (f32[256]{0:T(256)S(1)}, f32[256]{0:T(256)}, u32[]{:S(2)}) copy-start(f32[256]{0:T(256)} %param.20) | copy-start | bytes 3076
  73.6 7.4 %collective-permute-start.2 = (bf16[2,288,64]{1,0,2:T(2,128)(2,1)S(1)}, bf16[2,288,64]{1,0,2:T(2,128)(2,1)S(1)}, u32[]{:S(2)}, u32[]{:S(2)}) collective-permute-start(bf16[2,288,64]{1,0,2:T(2,128)(2,1)S(1)} %slice.212), channel_id=1, source_target_pairs={{0,1},{2,3},{4,5},{6,7},{8,9},{10,11},{12,13},{14,15},{16,17},{18,... | collective-permute-start | bytes 221192 | tf_op jit(solution)/shard_map/ppermute | solution.py:14
  76.0 5.0 %collective-permute-start.3 = (bf16[2,288,64]{1,0,2:T(2,128)(2,1)S(1)}, bf16[2,288,64]{1,0,2:T(2,128)(2,1)S(1)}, u32[]{:S(2)}, u32[]{:S(2)}) collective-permute-start(bf16[2,288,64]{1,0,2:T(2,128)(2,1)S(1)} %slice.214), channel_id=1, source_target_pairs={{1,0},{3,2},{5,4},{7,6},{9,8},{11,10},{13,12},{15,14},{17,16},{19,... | collective-permute-start | bytes 221192 | tf_op jit(solution)/shard_map/ppermute | solution.py:17
  94.7 7.0 %copy-start.27 = (bf16[36864]{0:T(1024)(128)(2,1)S(1)}, bf16[36864]{0:T(1024)(128)(2,1)}, u32[]{:S(2)}) copy-start(bf16[36864]{0:T(1024)(128)(2,1)} %reshape_reshape.4) | copy-start | bytes 221188
  94.7 7.0 %copy-start.39 = (bf16[64]{0:T(256)(128)(2,1)S(1)}, bf16[64]{0:T(256)(128)(2,1)}, u32[]{:S(2)}) copy-start(bf16[64]{0:T(256)(128)(2,1)} %convert.79) | copy-start | bytes 388
  94.7 7.0 %copy-start.40 = (bf16[64]{0:T(256)(128)(2,1)S(1)}, bf16[64]{0:T(256)(128)(2,1)}, u32[]{:S(2)}) copy-start(bf16[64]{0:T(256)(128)(2,1)} %convert.80) | copy-start | bytes 388
  94.7 7.0 %copy-start.41 = (bf16[256]{0:T(256)(128)(2,1)S(1)}, bf16[256]{0:T(256)(128)(2,1)}, u32[]{:S(2)}) copy-start(bf16[256]{0:T(256)(128)(2,1)} %convert.81) | copy-start | bytes 1540
  94.8 7.0 %copy-start.42 = (bf16[256]{0:T(256)(128)(2,1)S(1)}, bf16[256]{0:T(256)(128)(2,1)}, u32[]{:S(2)}) copy-start(bf16[256]{0:T(256)(128)(2,1)} %convert.82) | copy-start | bytes 1540
  94.8 13.3 %copy-start.1 = (f32[2304,256]{1,0:T(8,128)S(1)}, f32[2304,256]{1,0:T(8,128)}, u32[]{:S(2)}) copy-start(f32[2304,256]{1,0:T(8,128)} %get-tuple-element.45) | copy-start | bytes 7077892
  94.8 13.3 %copy-start.28 = (bf16[256,64]{0,1:T(8,128)(2,1)S(1)}, bf16[256,64]{0,1:T(8,128)(2,1)}, u32[]{:S(2)}) copy-start(bf16[256,64]{0,1:T(8,128)(2,1)} %param.12) | copy-start | bytes 98308
  (27 other events, 85.6 us)
Sparse Core Ops, SparseCore 0:
  108.2 20.3 all-reduce.8
where the time goes:
time: 223 us; the launch traced here: 222 us
  blocking collectives  106 us (48%)
  local copies, waits for them, and re-layouts  29.5 us (13%)
  matrix products  23.4 us (10%)
  other arithmetic  21.6 us (10%)
  waiting for transfers between devices  19 us (9%)
  between operations  15.8 us (7%)
  starting transfers between devices  7.13 us (3%)
    psum x1, blocking collectives, shards(): share = lax.psum(share, 'dp')  78.9 us
    unnamed x2, waiting for transfers between devices  19 us
    dot_general x18, matrix products, dilated(): jnp.dot(window, kernel[tap_row, tap_col], preferred_element_type=jnp.floa...  12.7 us
    reshape x16, local copies, waits for them, and re-layouts, dilated(): window = padded[2 * tap_row:2 * tap_row + rows, 2 * tap_col:2 * tap_col +...  12.4 us
    psum x3, blocking collectives, backnorm(): grad_sum, grad_cross = lax.psum((local_sum, local_cross), 'space')  8.68 us
    psum x3, blocking collectives, normalize(): average = lax.psum(jnp.sum(pre, 0), 'space') / count  8.36 us
    psum x3, blocking collectives, normalize(): variance = lax.psum(jnp.sum(centred * centred, 0), 'space') / count  7.59 us
    concatenate x1, local copies, waits for them, and re-layouts, shards(): flat_grads = jnp.concatenate([item.reshape(-1) for item in parts_list])  6.29 us
  transfers between devices with their start and end apart: 5, of which 1 were waited for; matrix products, arithmetic and copies ran while one was open for 3% of the time, Pallas kernels for 0%

commit v1 on v0

--- a/solution.py
+++ b/solution.py
@@ -4,6 +4,14 @@
 from jax.sharding import PartitionSpec as P
 
 epsilon = 1e-05
+
+
+def add_in_pairs(value, axis):
+    count, summed = (lax.axis_size(axis), value)
+    for reach in [1 << k for k in range(count.bit_length() - 1)]:
+        route = [(i, i ^ reach) for i in range(count)]
+        summed = summed + lax.ppermute(summed, axis, route)
+    return summed
 
 
 def extended(block, sides, width):
@@ -142,7 +150,7 @@
     share = lax.psum_scatter(
         flat_grads.astype(jnp.bfloat16), "space", scatter_dimension=0, tiled=True
     ).astype(jnp.float32)
-    share = lax.psum(share, "dp")
+    share = add_in_pairs(share, "dp")
     whole = lax.all_gather(share.astype(jnp.bfloat16), "space", axis=0, tiled=True).astype(
         share.dtype
     )

time: 223 us -> 168 us (0.75)
  blocking collectives: 106 us -> 25.9 us
  waiting for transfers between devices: 19 us -> 33.8 us
  starting transfers between devices: 7.13 us -> 15.6 us
    psum x1 -> x0, blocking collectives: 78.9 us -> none  [shards(): share = lax.psum(share, 'dp')]
    ppermute x0 -> x4, waiting for transfers between devices: none -> 14 us  [add_in_pairs(): summed = summed + lax.ppermute(summed, axis, route)]
    ppermute x0 -> x4, starting transfers between devices: none -> 8.44 us  [add_in_pairs(): summed = summed + lax.ppermute(summed, axis, route)]
  transfers between devices with their start and end apart: 5 -> 9, of which waited for: 1 -> 6; matrix products, arithmetic and copies ran while one was open for 3% -> 4% of each run, Pallas kernels for 0% -> 0%
where the time goes in v1:
time: 168 us; the launch traced here: 167 us
  waiting for transfers between devices  33.8 us (20%)
  local copies, waits for them, and re-layouts  29.6 us (18%)
  blocking collectives  25.9 us (15%)
  matrix products  23.4 us (14%)
  other arithmetic  22.7 us (14%)
  between operations  15.8 us (9%)
  starting transfers between devices  15.6 us (9%)
    unnamed x2, waiting for transfers between devices  19.2 us
    ppermute x4, waiting for transfers between devices, add_in_pairs(): summed = summed + lax.ppermute(summed, axis, route)  14 us
    dot_general x18, matrix products, dilated(): jnp.dot(window, kernel[tap_row, tap_col], preferred_element_type=jnp.floa...  12.7 us
    reshape x16, local copies, waits for them, and re-layouts, dilated(): window = padded[2 * tap_row:2 * tap_row + rows, 2 * tap_col:2 * tap_col +...  12.4 us
    psum x3, blocking collectives, backnorm(): grad_sum, grad_cross = lax.psum((local_sum, local_cross), 'space')  8.55 us
    ppermute x4, starting transfers between devices, add_in_pairs(): summed = summed + lax.ppermute(summed, axis, route)  8.44 us
    psum x3, blocking collectives, normalize(): average = lax.psum(jnp.sum(pre, 0), 'space') / count  7.79 us
    psum x3, blocking collectives, normalize(): variance = lax.psum(jnp.sum(centred * centred, 0), 'space') / count  7.59 us
  transfers between devices with their start and end apart: 9, of which 6 were waited for; matrix products, arithmetic and copies ran while one was open for 4% of the time, Pallas kernels for 0%

profile of v1, /device:TPU:0, one launch (start us, length us, event | category | flops | bytes accessed | tf_op | source)
XLA Modules:
  0.0 166.9 jit_solution(12652808267615334161)
XLA Ops:
  7.3 1.9 %fusion.60 = (f32[64]{0:T(128)S(1)}, f32[2304,64]{0,1:T(8,128)S(1)}) fusion(bf16[2304,256]{1,0:T(8,128)(2,1)} %bitcast.202, bf16[256,64]{0,1:T(8,128)(2,1)} %param.12), kind=kOutput, calls=%fused_computation.150 | convolution fusion | flops 75644864 | bytes 1802496 | tf_op jit(solution)/shard_map/dot_general | solution.py:95
  9.2 2.6 %psum.84 = f32[64]{0:T(128)S(1)} all-reduce(f32[64]{0:T(128)S(1)} %get-tuple-element.81), channel_id=1, replica_groups=mesh['dp'=16,'space'=2] {'space'}, use_global_device_ids=true, to_apply=%region_1.0 | all-reduce | flops 64 | bytes 512 | tf_op jit(solution)/shard_map/psum | solution.py:40
  12.1 2.5 %psum.85 = f32[64]{0:T(128)S(1)} all-reduce(f32[64]{0:T(128)S(1)} %multiply_reduce_fusion.5), channel_id=1, replica_groups=mesh['dp'=16,'space'=2] {'space'}, use_global_device_ids=true, to_apply=%region_3.0 | all-reduce | flops 64 | bytes 512 | tf_op jit(solution)/shard_map/psum | solution.py:42
  16.3 2.3 %collective-permute-start = (bf16[2,288,64]{1,0,2:T(2,128)(2,1)S(1)}, bf16[2,288,64]{1,0,2:T(2,128)(2,1)S(1)}, u32[]{:S(2)}, u32[]{:S(2)}) collective-permute-start(bf16[2,288,64]{1,0,2:T(2,128)(2,1)S(1)} %slice.191), channel_id=1, source_target_pairs={{0,1},{2,3},{4,5},{6,7},{8,9},{10,11},{12,13},{14,15},{16,17},{18,... | collective-permute-start | bytes 221192 | tf_op jit(solution)/shard_map/ppermute | solution.py:22
  41.5 2.7 %psum.86 = f32[64]{0:T(128)S(1)} all-reduce(f32[64]{0:T(128)S(1)} %get-tuple-element.83), channel_id=1, replica_groups=mesh['dp'=16,'space'=2] {'space'}, use_global_device_ids=true, to_apply=%region_5.6 | all-reduce | flops 64 | bytes 512 | tf_op jit(solution)/shard_map/psum | solution.py:40
  44.5 2.5 %psum.87 = f32[64]{0:T(128)S(1)} all-reduce(f32[64]{0:T(128)S(1)} %multiply_reduce_fusion.4), channel_id=1, replica_groups=mesh['dp'=16,'space'=2] {'space'}, use_global_device_ids=true, to_apply=%region_7.8 | all-reduce | flops 64 | bytes 512 | tf_op jit(solution)/shard_map/psum | solution.py:42
  47.0 1.9 %fusion.62 = (f32[256]{0:T(256)S(1)}, f32[2304,256]{1,0:T(8,128)S(1)}) fusion(bf16[64,256]{1,0:T(8,128)(2,1)S(1)} %copy-done, f32[2304,64]{0,1:T(8,128)} %copy-done.2, f32[64]{0:T(128)S(1)} %copy-done.44, f32[64]{0:T(128)S(1)} %get-tuple-element.80, f32[64]{0:T(128)S(1)} %broadcast_multiply_fusion.4, f32[64]{0:T(128)S(1)} %copy-done.43), kind=kOutput, calls=%fused_computation.152 | convolution fusion | flops 77414144 | bytes 2983936 | tf_op jit(solution)/shard_map/dot_general | solution.py:103
  48.8 2.5 %psum.88 = f32[256]{0:T(256)S(1)} all-reduce(f32[256]{0:T(256)S(1)} %get-tuple-element.85), channel_id=1, replica_groups=mesh['dp'=16,'space'=2] {'space'}, use_global_device_ids=true, to_apply=%region_9.10 | all-reduce | flops 256 | bytes 2048 | tf_op jit(solution)/shard_map/psum | solution.py:40
  51.7 2.6 %psum.89 = f32[256]{0:T(256)S(1)} all-reduce(f32[256]{0:T(256)S(1)} %multiply_reduce_fusion.1), channel_id=1, replica_groups=mesh['dp'=16,'space'=2] {'space'}, use_global_device_ids=true, to_apply=%region_11.12 | all-reduce | flops 256 | bytes 2048 | tf_op jit(solution)/shard_map/psum | solution.py:42
  54.3 5.1 %fusion.53 = (f32[256]{0:T(256)S(1)}, f32[256]{0:T(256)S(1)}, f32[2304,256]{1,0:T(8,128)}, bf16[2304,256]{1,0:T(8,128)(2,1)}) fusion(f32[256]{0:T(256)S(1)} %get-tuple-element.76, f32[2304,256]{1,0:T(8,128)S(1)} %get-tuple-element.86, f32[256]{0:T(256)S(1)} %broadcast_multiply_fusion.1, bf16[1,8,288,256]{3,2,1,0:T(8,128)(2,1)} %param.11, ...), kind=kLoop, calls=%fused_computation.143 | loop fusion | flops 11795968 | bytes 8263680 | tf_op jit(solution)/shard_map/reduce_sum | solution.py:49
  59.4 2.5 %all-reduce.5 = (f32[256]{0:T(256)S(1)}, f32[256]{0:T(256)S(1)}) all-reduce(f32[256]{0:T(256)S(1)} %get-tuple-element.34, f32[256]{0:T(256)S(1)} %get-tuple-element.33), channel_id=1, replica_groups=mesh['dp'=16,'space'=2] {'space'}, use_global_device_ids=true, to_apply=%region_15.16 | all-reduce | flops 512 | bytes 4096 | tf_op jit(solution)/shard_map/psum | solution.py:51
  61.9 2.3 %multiply_convert_fusion = bf16[2304,256]{1,0:T(8,128)(2,1)S(1)} fusion(f32[2304,256]{1,0:T(8,128)} %get-tuple-element.45, f32[2304,256]{1,0:T(8,128)S(1)} %get-tuple-element.86, f32[256]{0:T(256)S(1)} %get-tuple-element.43, f32[256]{0:T(256)S(1)} %broadcast_multiply_fusion, f32[256]{0:T(256)S(1)} %get-tuple-element.75, f32[256]{0:T(256)S(1)} %get-tuple-element.76, ...), kind=kLoop, calls=%fused_computation.23 | loop fusion | flops 4718592 | bytes 5903360 | tf_op jit(solution)/shard_map/convert_element_type | solution.py:52
  66.1 2.6 %all-reduce.4 = (f32[64]{0:T(128)S(1)}, f32[64]{0:T(128)S(1)}) all-reduce(f32[64]{0:T(128)S(1)} %get-tuple-element.38, f32[64]{0:T(128)S(1)} %get-tuple-element.37), channel_id=1, replica_groups=mesh['dp'=16,'space'=2] {'space'}, use_global_device_ids=true, to_apply=%region_19.20 | all-reduce | flops 128 | bytes 1024 | tf_op jit(solution)/shard_map/psum | solution.py:51
  72.4 2.3 %collective-permute-start.2 = (bf16[2,288,64]{1,0,2:T(2,128)(2,1)S(1)}, bf16[2,288,64]{1,0,2:T(2,128)(2,1)S(1)}, u32[]{:S(2)}, u32[]{:S(2)}) collective-permute-start(bf16[2,288,64]{1,0,2:T(2,128)(2,1)S(1)} %slice.212), channel_id=1, source_target_pairs={{0,1},{2,3},{4,5},{6,7},{8,9},{10,11},{12,13},{14,15},{16,17},{18,... | collective-permute-start | bytes 221192 | tf_op jit(solution)/shard_map/ppermute | solution.py:22
  93.6 3.5 %all-reduce.3 = (f32[64]{0:T(128)S(1)}, f32[64]{0:T(128)S(1)}) all-reduce(f32[64]{0:T(128)S(1)} %get-tuple-element.36, f32[64]{0:T(128)S(1)} %get-tuple-element.35), channel_id=1, replica_groups=mesh['dp'=16,'space'=2] {'space'}, use_global_device_ids=true, to_apply=%region_23.24 | all-reduce | flops 128 | bytes 1024 | tf_op jit(solution)/shard_map/psum | solution.py:51
  100.6 6.3 %concatenate.28 = bf16[70400]{0:T(1024)(128)(2,1)} concatenate(bf16[16384]{0:T(1024)(128)(2,1)S(1)} %reshape.180, bf16[36864]{0:T(1024)(128)(2,1)S(1)} %copy-done.27, bf16[16384]{0:T(1024)(128)(2,1)S(1)} %bitcast.206, bf16[64]{0:T(256)(128)(2,1)S(1)} %convert.77, bf16[64]{0:T(256)(128)(2,1)S(1)} %convert.78, bf16[64]{0:T(256)(128)(2,1)S(1)} %copy-done.39, ...), dimensions={0} | concatenate | bytes 281600 | tf_op jit(solution)/shard_map/concatenate | solution.py:145
  108.1 19.2 %all-reduce.8.cloned.1.call-done = bf16[70400]{0:T(1024)(128)(2,1)} async-done(((bf16[70400]{0:T(1024)(128)(2,1)}), bf16[70400]{0:T(1024)(128)(2,1)}) %all-reduce.8.cloned.1.call-update) | async-done | bytes 140816
  128.3 1.9 %collective-permute-start.4 = (f32[35200]{0:T(1024)S(1)}, f32[35200]{0:T(1024)S(1)}, u32[]{:S(2)}, u32[]{:S(2)}) collective-permute-start(f32[35200]{0:T(1024)S(1)} %dynamic-slice_convert_fusion), channel_id=1, source_target_pairs={{0,2},{2,0},{4,6},{6,4},{8,10},{10,8},{12,14},{14,12},{16,18},{18,... | collective-permute-start | bytes 422408 | tf_op jit(solution)/shard_map/ppermute | solution.py:13
  130.2 4.2 %collective-permute-done.4 = f32[35200]{0:T(1024)S(1)} collective-permute-done((f32[35200]{0:T(1024)S(1)}, f32[35200]{0:T(1024)S(1)}, u32[]{:S(2)}, u32[]{:S(2)}) %collective-permute-start.4) | collective-permute-done | bytes 140832 | tf_op jit(solution)/shard_map/ppermute | solution.py:13
  137.2 3.4 %collective-permute-done.5 = f32[35200]{0:T(1024)S(1)} collective-permute-done((f32[35200]{0:T(1024)S(1)}, f32[35200]{0:T(1024)S(1)}, u32[]{:S(2)}, u32[]{:S(2)}) %collective-permute-start.5) | collective-permute-done | bytes 140832 | tf_op jit(solution)/shard_map/ppermute | solution.py:13
  142.4 3.4 %collective-permute-done.6 = f32[35200]{0:T(1024)S(1)} collective-permute-done((f32[35200]{0:T(1024)S(1)}, f32[35200]{0:T(1024)S(1)}, u32[]{:S(2)}, u32[]{:S(2)}) %collective-permute-start.6) | collective-permute-done | bytes 140832 | tf_op jit(solution)/shard_map/ppermute | solution.py:13
  145.8 3.0 %collective-permute-start.7 = (f32[35200]{0:T(1024)S(1)}, f32[35200]{0:T(1024)S(1)}, u32[]{:S(2)}, u32[]{:S(2)}) collective-permute-start(f32[35200]{0:T(1024)S(1)} %add.189), channel_id=1, source_target_pairs={{0,16},{2,18},{4,20},{6,22},{8,24},{10,26},{12,28},{14,30},{16,0},... | collective-permute-start | bytes 422408 | tf_op jit(solution)/shard_map/ppermute | solution.py:13
  150.2 3.1 %collective-permute-done.7 = f32[35200]{0:T(1024)S(1)} collective-permute-done((f32[35200]{0:T(1024)S(1)}, f32[35200]{0:T(1024)S(1)}, u32[]{:S(2)}, u32[]{:S(2)}) %collective-permute-start.7) | collective-permute-done | bytes 140832 | tf_op jit(solution)/shard_map/ppermute | solution.py:13
  153.5 2.0 %all-gather = bf16[2,1,35200]{2,1,0:T(2,128)(2,1)S(1)} all-gather(bf16[1,1,35200]{2,1,0:T(2,128)(2,1)S(1)} %reshape.183), channel_id=1, replica_groups=mesh['dp'=16,'space'=2] {'space'}, dimensions={0}, use_global_device_ids=true | all-gather | bytes 211200 | tf_op jit(solution)/shard_map/all_gather | solution.py:154
  (206 shorter events, 65.2 us)
Async XLA Ops:
  7.2 39.8 %copy-start = (bf16[64,256]{1,0:T(8,128)(2,1)S(1)}, bf16[64,256]{1,0:T(8,128)(2,1)}, u32[]{:S(2)}) copy-start(bf16[64,256]{1,0:T(8,128)(2,1)} %param.14) | copy-start | bytes 98308
  7.2 7.3 %copy-start.34 = (f32[64]{0:T(128)S(1)}, f32[64]{0:T(128)}, u32[]{:S(2)}) copy-start(f32[64]{0:T(128)} %param.15) | copy-start | bytes 772
  7.2 8.4 %copy-start.37 = (f32[64]{0:T(128)S(1)}, f32[64]{0:T(128)}, u32[]{:S(2)}) copy-start(f32[64]{0:T(128)} %param.16) | copy-start | bytes 772
  7.2 13.4 %copy-start.25 = (bf16[3,3,64,64]{3,2,1,0:T(8,128)(2,1)S(1)}, bf16[3,3,64,64]{3,2,1,0:T(8,128)(2,1)}, u32[]{:S(2)}) copy-start(bf16[3,3,64,64]{3,2,1,0:T(8,128)(2,1)} %param.13) | copy-start | bytes 221188
  7.2 120.1 %all-reduce.8.cloned.1.call-start = ((), (), s32[]{:S(2)}) async-start(), calls=%async_computation | async-start | bytes 282624
  16.3 5.0 %collective-permute-start = (bf16[2,288,64]{1,0,2:T(2,128)(2,1)S(1)}, bf16[2,288,64]{1,0,2:T(2,128)(2,1)S(1)}, u32[]{:S(2)}, u32[]{:S(2)}) collective-permute-start(bf16[2,288,64]{1,0,2:T(2,128)(2,1)S(1)} %slice.191), channel_id=1, source_target_pairs={{0,1},{2,3},{4,5},{6,7},{8,9},{10,11},{12,13},{14,15},{16,17},{18,... | collective-permute-start | bytes 221192 | tf_op jit(solution)/shard_map/ppermute | solution.py:22
  18.7 3.2 %collective-permute-start.1 = (bf16[2,288,64]{1,0,2:T(2,128)(2,1)S(1)}, bf16[2,288,64]{1,0,2:T(2,128)(2,1)S(1)}, u32[]{:S(2)}, u32[]{:S(2)}) collective-permute-start(bf16[2,288,64]{1,0,2:T(2,128)(2,1)S(1)} %slice.193), channel_id=1, source_target_pairs={{1,0},{3,2},{5,4},{7,6},{9,8},{11,10},{13,12},{15,14},{17,16},{19,... | collective-permute-start | bytes 221192 | tf_op jit(solution)/shard_map/ppermute | solution.py:25
  39.3 7.6 %copy-start.43 = (f32[64]{0:T(128)S(1)}, f32[64]{0:T(128)}, u32[]{:S(2)}) copy-start(f32[64]{0:T(128)} %param.17) | copy-start | bytes 772
  39.3 7.6 %copy-start.44 = (f32[64]{0:T(128)S(1)}, f32[64]{0:T(128)}, u32[]{:S(2)}) copy-start(f32[64]{0:T(128)} %param.18) | copy-start | bytes 772
  47.0 7.4 %copy-start.33 = (f32[256]{0:T(256)S(1)}, f32[256]{0:T(256)}, u32[]{:S(2)}) copy-start(f32[256]{0:T(256)} %param.19) | copy-start | bytes 3076
  47.0 7.4 %copy-start.36 = (f32[256]{0:T(256)S(1)}, f32[256]{0:T(256)}, u32[]{:S(2)}) copy-start(f32[256]{0:T(256)} %param.20) | copy-start | bytes 3076
  72.4 7.4 %collective-permute-start.2 = (bf16[2,288,64]{1,0,2:T(2,128)(2,1)S(1)}, bf16[2,288,64]{1,0,2:T(2,128)(2,1)S(1)}, u32[]{:S(2)}, u32[]{:S(2)}) collective-permute-start(bf16[2,288,64]{1,0,2:T(2,128)(2,1)S(1)} %slice.212), channel_id=1, source_target_pairs={{0,1},{2,3},{4,5},{6,7},{8,9},{10,11},{12,13},{14,15},{16,17},{18,... | collective-permute-start | bytes 221192 | tf_op jit(solution)/shard_map/ppermute | solution.py:22
  74.8 5.0 %collective-permute-start.3 = (bf16[2,288,64]{1,0,2:T(2,128)(2,1)S(1)}, bf16[2,288,64]{1,0,2:T(2,128)(2,1)S(1)}, u32[]{:S(2)}, u32[]{:S(2)}) collective-permute-start(bf16[2,288,64]{1,0,2:T(2,128)(2,1)S(1)} %slice.214), channel_id=1, source_target_pairs={{1,0},{3,2},{5,4},{7,6},{9,8},{11,10},{13,12},{15,14},{17,16},{19,... | collective-permute-start | bytes 221192 | tf_op jit(solution)/shard_map/ppermute | solution.py:25
  93.5 7.0 %copy-start.27 = (bf16[36864]{0:T(1024)(128)(2,1)S(1)}, bf16[36864]{0:T(1024)(128)(2,1)}, u32[]{:S(2)}) copy-start(bf16[36864]{0:T(1024)(128)(2,1)} %reshape_reshape.4) | copy-start | bytes 221188
  93.5 7.0 %copy-start.39 = (bf16[64]{0:T(256)(128)(2,1)S(1)}, bf16[64]{0:T(256)(128)(2,1)}, u32[]{:S(2)}) copy-start(bf16[64]{0:T(256)(128)(2,1)} %convert.79) | copy-start | bytes 388
  93.5 7.0 %copy-start.40 = (bf16[64]{0:T(256)(128)(2,1)S(1)}, bf16[64]{0:T(256)(128)(2,1)}, u32[]{:S(2)}) copy-start(bf16[64]{0:T(256)(128)(2,1)} %convert.80) | copy-start | bytes 388
  93.5 7.0 %copy-start.41 = (bf16[256]{0:T(256)(128)(2,1)S(1)}, bf16[256]{0:T(256)(128)(2,1)}, u32[]{:S(2)}) copy-start(bf16[256]{0:T(256)(128)(2,1)} %convert.81) | copy-start | bytes 1540
  93.6 13.3 %copy-start.45 = (u32[32]{0:T(128)S(1)}, u32[32]{0:T(128)}, u32[]{:S(2)}) copy-start(u32[32]{0:T(128)} %constant.51) | copy-start | bytes 388
  97.1 51.6 %copy-start.1 = (f32[2304,256]{1,0:T(8,128)S(1)}, f32[2304,256]{1,0:T(8,128)}, u32[]{:S(2)}) copy-start(f32[2304,256]{1,0:T(8,128)} %get-tuple-element.45) | copy-start | bytes 7077892
  97.1 51.6 %copy-start.28 = (bf16[256,64]{0,1:T(8,128)(2,1)S(1)}, bf16[256,64]{0,1:T(8,128)(2,1)}, u32[]{:S(2)}) copy-start(bf16[256,64]{0,1:T(8,128)(2,1)} %param.12) | copy-start | bytes 98308
  128.3 6.0 %collective-permute-start.4 = (f32[35200]{0:T(1024)S(1)}, f32[35200]{0:T(1024)S(1)}, u32[]{:S(2)}, u32[]{:S(2)}) collective-permute-start(f32[35200]{0:T(1024)S(1)} %dynamic-slice_convert_fusion), channel_id=1, source_target_pairs={{0,2},{2,0},{4,6},{6,4},{8,10},{10,8},{12,14},{14,12},{16,18},{18,... | collective-permute-start | bytes 422408 | tf_op jit(solution)/shard_map/ppermute | solution.py:13
  135.4 5.2 %collective-permute-start.5 = (f32[35200]{0:T(1024)S(1)}, f32[35200]{0:T(1024)S(1)}, u32[]{:S(2)}, u32[]{:S(2)}) collective-permute-start(f32[35200]{0:T(1024)S(1)} %fusion.26), channel_id=1, source_target_pairs={{0,4},{2,6},{4,0},{6,2},{8,12},{10,14},{12,8},{14,10},{16,20},{18,... | collective-permute-start | bytes 422408 | tf_op jit(solution)/shard_map/ppermute | solution.py:13
  140.6 5.2 %collective-permute-start.6 = (f32[35200]{0:T(1024)S(1)}, f32[35200]{0:T(1024)S(1)}, u32[]{:S(2)}, u32[]{:S(2)}) collective-permute-start(f32[35200]{0:T(1024)S(1)} %add.188), channel_id=1, source_target_pairs={{0,8},{2,10},{4,12},{6,14},{8,0},{10,2},{12,4},{14,6},{16,24},{18,... | collective-permute-start | bytes 422408 | tf_op jit(solution)/shard_map/ppermute | solution.py:13
  145.8 7.6 %collective-permute-start.7 = (f32[35200]{0:T(1024)S(1)}, f32[35200]{0:T(1024)S(1)}, u32[]{:S(2)}, u32[]{:S(2)}) collective-permute-start(f32[35200]{0:T(1024)S(1)} %add.189), channel_id=1, source_target_pairs={{0,16},{2,18},{4,20},{6,22},{8,24},{10,26},{12,28},{14,30},{16,0},... | collective-permute-start | bytes 422408 | tf_op jit(solution)/shard_map/ppermute | solution.py:13
  (31 other events, 109.8 us)
Sparse Core Ops, SparseCore 0:
  107.0 20.3 all-reduce.7
